TPU v7x, 32 devices: a whole 2x2x4 slice. The times are simulated.
32 devices in a mesh: dp: 16 (over z, y, x), mp: 2 (over core).
Axes of the slice: x: 2, y: 2, z: 4, core: 2. Of those that a mesh axis runs over, the one named last changes fastest.
Arguments:
- tokens: bfloat16 [8192, 2048], P('dp'), may hold values from -6 to 6
- noise_cond: float32 [128, 8192], P('dp'), may hold values from -1.5 to 1.5
- slot_bucket: int32 [16], P('dp'), may hold values from 0 to 3, as said below
- image_height: int32 [16, 8], P('dp'), may hold values from 5 to 16, as said below
- image_width: int32 [16, 8], P('dp'), may hold values from 5 to 32, as said below
- weight_query: bfloat16 [2048, 2048], P('dp', 'mp'), may hold values from -0.1875 to 0.1875
- weight_key: bfloat16 [2048, 2048], P('dp', 'mp'), may hold values from -0.1875 to 0.1875
- weight_value: bfloat16 [2048, 2048], P('dp', 'mp'), may hold values from -0.125 to 0.125
- weight_out: bfloat16 [2048, 2048], P('mp', 'dp'), may hold values from -0.5 to 0.5
- weight_in: bfloat16 [2048, 8192], P('dp', 'mp'), may hold values from -0.125 to 0.125
- weight_back: bfloat16 [8192, 2048], P('mp', 'dp'), may hold values from -0.09375 to 0.09375
- cotangent: bfloat16 [8192, 2048], P('dp'), may hold values from -6 to 6
Outputs:
- block_output: bfloat16 [8192, 2048], P('dp')
- grad_tokens: float32 [8192, 2048], P('dp')
- grad_cond: float32 [128, 8192], P('dp')
- grad_query: float32 [2048, 2048], P('dp', 'mp')
- grad_key: float32 [2048, 2048], P('dp', 'mp')
- grad_value: float32 [2048, 2048], P('dp', 'mp')
- grad_out: float32 [2048, 2048], P('mp', 'dp')
- grad_in: float32 [2048, 8192], P('dp', 'mp')
- grad_back: float32 [8192, 2048], P('mp', 'dp')
Inputs may be any that keep to these rules, and one draw needn't show every extreme that they name: `slot_bucket`: buckets 0 to 3 hold 8, 4, 2, 1 images of a slot; the first slot is of bucket 3. `image_height`: greater than half of the bucket's grid height and at most it: 8 for buckets 0 and 1, 16 for buckets 2 and 3; entries of images past the slot's count are unused. `image_width`: greater than half of the bucket's grid width and at most it: 8, 16, 16, 32 for buckets 0 to 3; entries of images past the slot's count are unused.
All inputs are finite; a program needn't handle non-finite values.
Results may differ from a plain program's by a relative error of at most 0.014.
Values may be sent and summed in bfloat16 or wider, within the bound.
No kernel may reach another device: no remote copies, remote signals or barrier semaphores. Data moves between devices by JAX's collectives and lax.ppermute only.
A program may use at most 384 MiB of HBM per device.

v0:
```python
import jax
import jax.numpy as jnp
from jax import lax
from jax.sharding import Mesh, PartitionSpec as P

HD = 128
GW = 32
IMG_SLOT = 8
SLOT = 512
HALF = SLOT // 2
EPS = 1e-06
HIGH = lax.Precision.HIGHEST
BF = jnp.bfloat16
F32 = jnp.float32
PAIRED = (0, 4, 1, 6, 2, 5, 3, 7)
UNPAIRED = (0, 2, 4, 6, 1, 5, 3, 7)


def arrange(slot_bucket, image_height, image_width, places):
    choose = (slot_bucket[:, None] == jnp.arange(4, dtype=jnp.int32)[None, :]).astype(jnp.int32)
    areas = jnp.sum(
        choose * jnp.array([SLOT // 8, SLOT // 4, SLOT // 2, SLOT], jnp.int32)[None, :], axis=1
    )
    across = jnp.sum(
        choose * jnp.array([GW // 4, GW // 2, GW // 2, GW], jnp.int32)[None, :], axis=1
    )
    image = places[None, :] // areas[:, None]
    inner = places[None, :] % areas[:, None]
    grid_row = inner // across[:, None]
    grid_col = inner % across[:, None]
    member = image[:, :, None] == jnp.arange(IMG_SLOT, dtype=jnp.int32)[None, None, :]
    tall = jnp.sum(jnp.where(member, image_height[:, None, :], 0), axis=2)
    broad = jnp.sum(jnp.where(member, image_width[:, None, :], 0), axis=2)
    real = (grid_row < tall) & (grid_col < broad)
    return (image, real)


def modulate(hidden, member, cond_part):
    width = hidden.shape[-1]
    mods = jnp.einsum("ti,ic->tc", member, cond_part, precision=HIGH)
    factor = lax.rsqrt(jnp.mean(hidden * hidden, axis=-1, keepdims=True) + EPS)
    return hidden * factor * (1.0 + mods[:, :width]) + mods[:, width:]


def contract_rows(left, right):
    return lax.dot_general(left, right, (((0,), (0,)), ((), ())), preferred_element_type=F32)


def times_transposed(left, right):
    return lax.dot_general(left, right, (((1,), (1,)), ((), ())), preferred_element_type=F32)


def times(left, right):
    return jnp.dot(left, right, preferred_element_type=F32)


def reorder(rows, order):
    blocks = rows.reshape(8, HALF, rows.shape[-1])
    return jnp.concatenate([blocks[i] for i in order], axis=0)


def heads_of(rows):
    return rows.reshape(4, SLOT, -1, HD)


def attend_forward(queries, keys_low, values, allowed):
    scores = jnp.einsum("sqhd,skhd->shqk", queries, keys_low, preferred_element_type=F32) * HD ** (
        -0.5
    )
    scores = jnp.where(allowed, scores, -1e30)
    top = jnp.max(scores, axis=-1, keepdims=True)
    weights = jnp.where(allowed, jnp.exp(scores - top), 0.0)
    total = jnp.sum(weights, axis=-1, keepdims=True)
    probs = (weights / total).astype(BF)
    mixed = jnp.einsum("shqk,skhd->sqhd", probs, values, preferred_element_type=F32)
    return (mixed.astype(BF).reshape(4 * SLOT, -1), top + jnp.log(total))


def attend_backward(queries, keys_low, values, allowed, logsum, grad_mixed):
    scale = HD ** (-0.5)
    scores = jnp.einsum("sqhd,skhd->shqk", queries, keys_low, preferred_element_type=F32) * scale
    probs = jnp.where(allowed, jnp.exp(scores - logsum), 0.0)
    grad_values = jnp.einsum(
        "shqk,sqhd->skhd", probs.astype(BF), grad_mixed, preferred_element_type=F32
    )
    grad_probs = jnp.einsum("sqhd,skhd->shqk", grad_mixed, values, preferred_element_type=F32)
    grad_scores = probs * (grad_probs - jnp.sum(probs * grad_probs, axis=-1, keepdims=True))
    grad_scores = grad_scores.astype(BF)
    grad_queries = (
        jnp.einsum("shqk,skhd->sqhd", grad_scores, keys_low, preferred_element_type=F32) * scale
    )
    grad_keys = (
        jnp.einsum("shqk,sqhd->skhd", grad_scores, queries, preferred_element_type=F32) * scale
    )
    return tuple(
        (part.astype(BF).reshape(4 * SLOT, -1) for part in (grad_queries, grad_keys, grad_values))
    )


def solution(mesh):
    outer = mesh.shape["dp"] // 4
    inner_mesh = Mesh(mesh.devices.reshape(outer, 2, 2, 2), ("o", "y", "x", "mp"))
    every = ("o", "y", "x", "mp")

    def pairs(move):
        made = []
        for o in range(outer):
            for y in range(2):
                for x in range(2):
                    for m in range(2):
                        ty, tx, tm = move(y, x, m)
                        made.append(
                            (((o * 2 + y) * 2 + x) * 2 + m, ((o * 2 + ty) * 2 + tx) * 2 + tm)
                        )
        return made

    near = pairs(lambda y, x, m: (y, 1 - x, m) if m == 0 else (1 - y, x, m))
    next_near = pairs(lambda y, x, m: (1 - y, x, m) if m == 0 else (y, 1 - x, m))
    sibling = pairs(lambda y, x, m: (y, x, 1 - m))
    offsets = {k: pairs(lambda y, x, m, k=k: (y ^ k >> 1, x ^ k & 1, m)) for k in (1, 2, 3)}

    def move(value, how):
        return lax.ppermute(value, every, how)

    def gather_rows(own):
        first = jnp.concatenate([own, move(own, near)], axis=0)
        second = move(first, next_near)
        return jnp.concatenate([first, second, move(first, sibling), move(second, sibling)], axis=0)

    def scatter_rows(left, right):
        quarter = left.shape[0] // 4

        def part(i):
            return times_transposed(left[i * quarter : (i + 1) * quarter], right)

        far = part(1) + move(part(3).astype(BF), sibling).astype(F32)
        got = move(far.astype(BF), next_near)
        close = part(0) + move(part(2).astype(BF), sibling).astype(F32)
        close = close + got.astype(F32)
        return close[:HALF] + move(close[HALF:].astype(BF), near).astype(F32)

    def spread_weight(shard, blocks):
        rows = shard.shape[0]
        chip = lax.axis_index("y") * 2 + lax.axis_index("x")
        parts = shard.reshape(rows, blocks, 4, -1)
        width = parts.shape[-1]
        gathered = jnp.zeros((4, rows, blocks * width), shard.dtype)
        for k in range(4):
            there = chip ^ k
            piece = lax.dynamic_index_in_dim(parts, there, 2, keepdims=False)
            piece = piece.reshape(rows, blocks * width)
            if k:
                piece = move(piece, offsets[k])
            gathered = lax.dynamic_update_slice(gathered, piece[None], (there, 0, 0))
        gathered = gathered.reshape(4 * rows, blocks * width)
        return lax.all_gather(gathered, "o", axis=0, tiled=True)

    def collect_grad(partial, blocks):
        mine = lax.psum_scatter(partial, "o", scatter_dimension=0, tiled=True)
        chip = lax.axis_index("y") * 2 + lax.axis_index("x")
        rows = mine.shape[0] // 4
        width = mine.shape[1] // blocks
        mine = mine.reshape(4, rows, blocks, 1, width)
        result = jnp.zeros((rows, blocks, 4, width), F32)
        for k in range(4):
            there = chip ^ k
            piece = lax.dynamic_index_in_dim(mine, there, 0, keepdims=False)
            if k:
                piece = move(piece, offsets[k])
            result = lax.dynamic_update_slice(result, piece, (0, 0, there, 0))
        return result.reshape(rows, blocks, 4 * width)

    def local(
        tokens,
        noise_cond,
        slot_bucket,
        image_height,
        image_width,
        weight_query,
        weight_key,
        weight_value,
        weight_out,
        weight_in,
        weight_back,
        cotangent,
    ):
        core = lax.axis_index("mp")
        width = tokens.shape[1]
        places = (jnp.arange(SLOT, dtype=jnp.int32) + HALF * core) % SLOT
        facts = jnp.concatenate([slot_bucket[:, None], image_height, image_width], axis=1)
        facts = jnp.concatenate([facts, move(facts, near)], axis=0)
        facts = jnp.concatenate([facts, move(facts, next_near)], axis=0)
        image, real = arrange(
            facts[:, 0], facts[:, 1 : 1 + IMG_SLOT], facts[:, 1 + IMG_SLOT :], places
        )
        allowed = ((image[:, :, None] == image[:, None, :]) & real[:, None, :])[:, None]
        member = (image[0, :HALF, None] == jnp.arange(IMG_SLOT, dtype=jnp.int32)[None, :]).astype(
            F32
        )
        first_cond = noise_cond[:, : 2 * width]
        second_cond = noise_cond[:, 2 * width :]
        qkv_full = spread_weight(
            jnp.concatenate([weight_query, weight_key, weight_value], axis=1), 3
        )
        out_full = spread_weight(weight_out.T, 1)
        in_full = spread_weight(weight_in, 1)
        back_full = spread_weight(weight_back.T, 1)
        hidden = lax.dynamic_slice(tokens, (core * HALF, 0), (HALF, width)).astype(F32)
        grad_result = lax.dynamic_slice(cotangent, (core * HALF, 0), (HALF, width))
        first = gather_rows(modulate(hidden, member, first_cond).astype(BF))
        cotangents = gather_rows(grad_result)
        qkv = reorder(times(first, qkv_full).astype(BF), PAIRED)
        part = qkv.shape[1] // 3
        queries, keys_low, values = (heads_of(qkv[:, i * part : (i + 1) * part]) for i in range(3))
        attended, logsum = attend_forward(queries, keys_low, values, allowed)
        attended = reorder(attended, UNPAIRED)
        middle = hidden + scatter_rows(attended, out_full)
        second = gather_rows(modulate(middle, member, second_cond).astype(BF))
        before = times(second, in_full)

        def gelu_exact(pre_act):
            return jax.nn.gelu(pre_act, approximate=False)

        after, gelu_pullback = jax.vjp(gelu_exact, before)
        after = after.astype(BF)
        grad_back = collect_grad(contract_rows(cotangents, after), 1)
        grad_before = gelu_pullback(times(cotangents, back_full))[0].astype(BF)
        grad_in = collect_grad(contract_rows(second, grad_before), 1)
        grad_second = scatter_rows(grad_before, in_full)
        result = (middle + scatter_rows(after, back_full)).astype(BF)

        def norm(rows_in, cond_in):
            return modulate(rows_in, member, cond_in)

        unused, second_pullback = jax.vjp(norm, middle, second_cond)
        grad_middle_norm, grad_second_cond = second_pullback(grad_second)
        grad_middle = grad_result.astype(F32) + grad_middle_norm
        grad_branch = gather_rows(grad_middle.astype(BF))
        grad_out = collect_grad(contract_rows(grad_branch, attended), 1)
        grad_attended = reorder(times(grad_branch, out_full).astype(BF), PAIRED)
        grad_qkv = attend_backward(
            queries, keys_low, values, allowed, logsum, heads_of(grad_attended)
        )
        grad_qkv = reorder(jnp.concatenate(grad_qkv, axis=1), UNPAIRED)
        grad_qkv_weight = collect_grad(contract_rows(first, grad_qkv), 3)
        grad_first = scatter_rows(grad_qkv, qkv_full)
        unused, first_pullback = jax.vjp(norm, hidden, first_cond)
        grad_hidden_norm, grad_first_cond = first_pullback(grad_first)
        grad_tokens = grad_middle + grad_hidden_norm
        grad_cond = jnp.concatenate([grad_first_cond, grad_second_cond], axis=1)
        grad_cond = grad_cond + move(grad_cond, sibling)

        def both_halves(rows):
            other = move(rows, sibling)
            made = jnp.zeros((SLOT, width), rows.dtype)
            made = lax.dynamic_update_slice(made, rows, (core * HALF, 0))
            return lax.dynamic_update_slice(made, other, ((1 - core) * HALF, 0))

        return (
            both_halves(result),
            both_halves(grad_tokens),
            grad_cond,
            grad_qkv_weight[:, 0],
            grad_qkv_weight[:, 1],
            grad_qkv_weight[:, 2],
            grad_out[:, 0].T,
            grad_in[:, 0],
            grad_back[:, 0].T,
        )

    dp = ("o", "y", "x")
    return jax.shard_map(
        local,
        mesh=inner_mesh,
        in_specs=(
            P(dp, None),
            P(dp, None),
            P(dp),
            P(dp, None),
            P(dp, None),
            P(dp, "mp"),
            P(dp, "mp"),
            P(dp, "mp"),
            P("mp", dp),
            P(dp, "mp"),
            P("mp", dp),
            P(dp, None),
        ),
        out_specs=(
            P(dp, None),
            P(dp, None),
            P(dp, None),
            P(dp, "mp"),
            P(dp, "mp"),
            P(dp, "mp"),
            P("mp", dp),
            P(dp, "mp"),
            P("mp", dp),
        ),
        check_vma=False,
    )
```

profile of v0, /device:TPU:0, one launch (start us, length us, event | category | flops | bytes accessed | tf_op | source)
XLA Modules:
  0.0 1036.5 jit_solution(10898821490958238784)
XLA Ops:
  40.4 9.0 collective-permute-done.2
  55.9 22.7 %collective-permute-done.3 = bf16[512,2048]{1,0:T(8,128)(2,1)} collective-permute-done((bf16[512,2048]{1,0:T(8,128)(2,1)}, bf16[512,2048]{1,0:T(8,128)(2,1)}, u32[]{:S(2)}, u32[]{:S(2)}) %collective-permute-start.3) | collective-permute-done | bytes 2097184 | tf_op jit(solution)/shard_map/ppermute | solution.py:123
  92.9 11.5 %all-gather.5.cloned.1.call-done = bf16[2048,768]{1,0:T(8,128)(2,1)} async-done(((bf16[512,768]{1,0:T(8,128)(2,1)}), bf16[2048,768]{1,0:T(8,128)(2,1)}) %all-gather.5.cloned.1.call-update) | async-done | bytes 3145744 | tf_op jit(solution)/shard_map/all_gather | solution.py:156
  104.4 10.0 convolution_convert_fusion
  160.3 20.7 %collective-permute-done.14 = bf16[512,2048]{1,0:T(8,128)(2,1)} collective-permute-done((bf16[512,2048]{1,0:T(8,128)(2,1)}, bf16[512,2048]{1,0:T(8,128)(2,1)}, u32[]{:S(2)}, u32[]{:S(2)}) %collective-permute-start.14) | collective-permute-done | bytes 2097184 | tf_op jit(solution)/shard_map/ppermute | solution.py:123
  189.9 9.6 collective-permute-done.15
  203.4 7.4 collective-permute-done.31
  227.3 8.8 collective-permute-done.23
  241.9 9.2 collective-permute-done.24
  254.6 7.1 collective-permute-start.33
  262.2 14.2 %collective-permute-done.17 = bf16[512,2048]{1,0:T(8,128)(2,1)} collective-permute-done((bf16[512,2048]{1,0:T(8,128)(2,1)}, bf16[512,2048]{1,0:T(8,128)(2,1)}, u32[]{:S(2)}, u32[]{:S(2)}) %collective-permute-start.17) | collective-permute-done | bytes 2097184 | tf_op jit(solution)/shard_map/ppermute | solution.py:123
  276.4 6.6 collective-permute-start.19
  299.9 14.9 %fusion.132 = f32[2048,1024]{1,0:T(8,128)} fusion(bf16[2048,2048]{1,0:T(8,128)(2,1)} %constant_dynamic-update-slice_fusion.5, bf16[2048,1024]{1,0:T(8,128)(2,1)} %all-gather.9.cloned.1.call-done), kind=kOutput, calls=%fused_computation.344 | convolution fusion | flops 8589934592 | bytes 20971520 | tf_op jit(solution)/shard_map/dot_general | solution.py:54
  314.9 25.5 %all-gather.11.cloned.1.call-done = bf16[2048,1024]{1,0:T(8,128)(2,1)} async-done(((bf16[512,1024]{1,0:T(8,128)(2,1)}), bf16[2048,1024]{1,0:T(8,128)(2,1)}) %all-gather.11.cloned.1.call-update) | async-done | bytes 4194320 | tf_op jit(solution)/shard_map/all_gather | solution.py:156
  340.3 32.3 %add_convert_fusion = (bf16[2048,1024]{1,0:T(8,128)(2,1)S(1)}, f32[2048,1024]{1,0:T(8,128)}) fusion(f32[2048,1024]{1,0:T(8,128)} %fusion.132, bf16[2048,2048]{1,0:T(8,128)(2,1)} %constant_dynamic-update-slice_fusion.10, bf16[2048,1024]{1,0:T(8,128)(2,1)} %all-gather.11.cloned.1.call-done), kind=kOutput, calls=%fused_computation.5 | convolution fusion | flops 8740929536 | bytes 33554432 | tf_op jit(solution)/shard_map/dot_general | solution.py:54
  376.4 10.2 multiply_convert_fusion.1
  416.1 11.6 %collective-permute-done.37 = bf16[512,2048]{1,0:T(8,128)(2,1)S(1)} collective-permute-done((bf16[512,2048]{1,0:T(8,128)(2,1)}, bf16[512,2048]{1,0:T(8,128)(2,1)S(1)}, u32[]{:S(2)}, u32[]{:S(2)}) %collective-permute-start.37) | collective-permute-done | bytes 2097184 | tf_op jit(solution)/shard_map/ppermute | solution.py:123
  432.9 28.5 %collective-permute-done.28 = bf16[512,2048]{1,0:T(8,128)(2,1)S(1)} collective-permute-done((bf16[512,2048]{1,0:T(8,128)(2,1)}, bf16[512,2048]{1,0:T(8,128)(2,1)S(1)}, u32[]{:S(2)}, u32[]{:S(2)}) %collective-permute-start.28) | collective-permute-done | bytes 2097184 | tf_op jit(solution)/shard_map/ppermute | solution.py:123
  466.7 10.7 %collective-permute-done.29 = bf16[256,2048]{1,0:T(8,128)(2,1)S(1)} collective-permute-done((bf16[256,2048]{1,0:T(8,128)(2,1)S(1)}, bf16[256,2048]{1,0:T(8,128)(2,1)S(1)}, u32[]{:S(2)}, u32[]{:S(2)}) %collective-permute-start.29) | collective-permute-done | bytes 1048608 | tf_op jit(solution)/shard_map/ppermute | solution.py:123
  482.2 13.3 %collective-permute-done.39 = bf16[256,2048]{1,0:T(8,128)(2,1)S(1)} collective-permute-done((bf16[256,2048]{1,0:T(8,128)(2,1)S(1)}, bf16[256,2048]{1,0:T(8,128)(2,1)S(1)}, u32[]{:S(2)}, u32[]{:S(2)}) %collective-permute-start.39) | collective-permute-done | bytes 1048608 | tf_op jit(solution)/shard_map/ppermute | solution.py:123
  497.4 24.4 %collective-permute-done.40 = bf16[512,2048]{1,0:T(8,128)(2,1)S(1)} collective-permute-done((bf16[512,2048]{1,0:T(8,128)(2,1)S(1)}, bf16[512,2048]{1,0:T(8,128)(2,1)S(1)}, u32[]{:S(2)}, u32[]{:S(2)}) %collective-permute-start.40) | collective-permute-done | bytes 2097184 | tf_op jit(solution)/shard_map/ppermute | solution.py:123
  527.8 7.3 fusion.134
  535.1 14.7 %fusion.135 = f32[2048,1024]{1,0:T(8,128)} fusion(bf16[2048,2048]{1,0:T(8,128)(2,1)} %constant_dynamic-update-slice_fusion.5, bf16[2048,1024]{1,0:T(8,128)(2,1)} %copy-done.75), kind=kOutput, calls=%fused_computation.347 | convolution fusion | flops 8589934592 | bytes 20971520 | tf_op jit(solution)/shard_map/dot_general | solution.py:46
  549.9 14.7 %fusion.136 = f32[2048,1024]{1,0:T(8,128)} fusion(bf16[2048,2048]{1,0:T(8,128)(2,1)} %constant_dynamic-update-slice_fusion.10, bf16[2048,1024]{1,0:T(8,128)(2,1)} %multiply_convert_fusion.1), kind=kOutput, calls=%fused_computation.348 | convolution fusion | flops 8589934592 | bytes 20971520 | tf_op jit(solution)/shard_map/dot_general | solution.py:46
  573.2 6.8 fusion.40
  609.6 9.1 fusion.133
  635.4 21.0 %collective-permute-done.45 = bf16[512,2048]{1,0:T(8,128)(2,1)} collective-permute-done((bf16[512,2048]{1,0:T(8,128)(2,1)}, bf16[512,2048]{1,0:T(8,128)(2,1)}, u32[]{:S(2)}, u32[]{:S(2)}) %collective-permute-start.45) | collective-permute-done | bytes 2097184 | tf_op jit(solution)/shard_map/ppermute | solution.py:123
  673.9 7.9 collective-permute-done.52
  694.1 29.4 %reduce-scatter.9.cloned.1.call-done = f32[512,1024]{1,0:T(8,128)} async-done(((f32[2048,1024]{1,0:T(8,128)}), f32[512,1024]{1,0:T(8,128)}) %reduce-scatter.9.cloned.1.call-update) | async-done | bytes 2097168 | tf_op jit(solution)/shard_map/reduce_scatter | solution.py:159
  734.4 136.8 %reduce-scatter.11.cloned.1.call-done = f32[512,1024]{1,0:T(8,128)} async-done(((f32[2048,1024]{1,0:T(8,128)}), f32[512,1024]{1,0:T(8,128)}) %reduce-scatter.11.cloned.1.call-update) | async-done | bytes 2097168 | tf_op jit(solution)/shard_map/reduce_scatter | solution.py:159
  899.7 11.3 %collective-permute-done.57 = f32[128,1,1,1024]{3,0,2,1:T(8,128)} collective-permute-done((f32[128,1,1,1024]{3,0,2,1:T(8,128)}, f32[128,1,1,1024]{3,0,2,1:T(8,128)}, u32[]{:S(2)}, u32[]{:S(2)}) %collective-permute-start.57) | collective-permute-done | bytes 524320 | tf_op jit(solution)/shard_map/ppermute | solution.py:123
  925.9 59.0 %reduce-scatter.5.cloned.1.call-done = f32[512,768]{1,0:T(8,128)} async-done(((f32[2048,768]{1,0:T(8,128)}), f32[512,768]{1,0:T(8,128)}) %reduce-scatter.5.cloned.1.call-update) | async-done | bytes 1572880 | tf_op jit(solution)/shard_map/reduce_scatter | solution.py:159
  (516 shorter events, 393.2 us)
Async XLA Ops:
  7.2 97.2 %all-gather.5.cloned.1.call-start = ((), (), s32[]{:S(2)}) async-start(), calls=%async_computation.4 | async-start | bytes 3932160 | tf_op jit(solution)/shard_map/all_gather | solution.py:156
  40.4 96.1 %all-gather.7.cloned.1.call-start = ((), (), s32[]{:S(2)}) async-start(), calls=%async_computation.5 | async-start | bytes 1310720 | tf_op jit(solution)/shard_map/all_gather | solution.py:156
  50.9 27.8 %collective-permute-start.3 = (bf16[512,2048]{1,0:T(8,128)(2,1)}, bf16[512,2048]{1,0:T(8,128)(2,1)}, u32[]{:S(2)}, u32[]{:S(2)}) collective-permute-start(bf16[512,2048]{1,0:T(8,128)(2,1)} %pad_maximum_fusion), channel_id=1, source_target_pairs={{0,4},{1,3},{2,6},{3,1},{4,0},{5,7},{6,2},{7,5},{8,12},{9,11},{10,... | collective-permute-start | bytes 6291464 | tf_op jit(solution)/shard_map/ppermute | solution.py:123
  51.0 30.0 %collective-permute-start.9 = (bf16[128,256]{1,0:T(8,128)(2,1)S(1)}, bf16[128,256]{1,0:T(8,128)(2,1)S(1)}, u32[]{:S(2)}, u32[]{:S(2)}) collective-permute-start(bf16[128,256]{1,0:T(8,128)(2,1)S(1)} %bitcast.250), channel_id=1, source_target_pairs={{0,2},{1,3},{2,0},{3,1},{4,6},{5,7},{6,4},{7,5},{8,10},{9,11},{10,... | collective-permute-start | bytes 196616 | tf_op jit(solution)/shard_map/ppermute | solution.py:123
  51.7 29.4 %collective-permute-start.10 = (bf16[128,256]{1,0:T(8,128)(2,1)S(1)}, bf16[128,256]{1,0:T(8,128)(2,1)S(1)}, u32[]{:S(2)}, u32[]{:S(2)}) collective-permute-start(bf16[128,256]{1,0:T(8,128)(2,1)S(1)} %bitcast.249), channel_id=1, source_target_pairs={{0,4},{1,5},{2,6},{3,7},{4,0},{5,1},{6,2},{7,3},{8,12},{9,13},{10,... | collective-permute-start | bytes 196616 | tf_op jit(solution)/shard_map/ppermute | solution.py:123
  55.1 31.3 %collective-permute-start.4 = (bf16[512,2048]{1,0:T(8,128)(2,1)}, bf16[512,2048]{1,0:T(8,128)(2,1)}, u32[]{:S(2)}, u32[]{:S(2)}) collective-permute-start(bf16[512,2048]{1,0:T(8,128)(2,1)} %pad_maximum_fusion), channel_id=1, source_target_pairs={{0,1},{1,0},{2,3},{3,2},{4,5},{5,4},{6,7},{7,6},{8,9},{9,8},{10,11... | collective-permute-start | bytes 6291464 | tf_op jit(solution)/shard_map/ppermute | solution.py:123
  82.0 218.0 %all-gather.9.cloned.1.call-start = ((), (), s32[]{:S(2)}) async-start(), calls=%async_computation.6 | async-start | bytes 5242880 | tf_op jit(solution)/shard_map/all_gather | solution.py:156
  159.5 180.9 %all-gather.11.cloned.1.call-start = ((), (), s32[]{:S(2)}) async-start(), calls=%async_computation.7 | async-start | bytes 5242880 | tf_op jit(solution)/shard_map/all_gather | solution.py:156
  202.4 35.3 %collective-permute-start.16 = (bf16[256,2048]{1,0:T(8,128)(2,1)S(1)}, bf16[256,2048]{1,0:T(8,128)(2,1)}, u32[]{:S(2)}, u32[]{:S(2)}) collective-permute-start(bf16[256,2048]{1,0:T(8,128)(2,1)S(1)} %get-tuple-element.29), channel_id=1, source_target_pairs={{0,2},{1,5},{2,0},{3,7},{4,6},{5,1},{6,4},{7,3},{8,10},{9,13},{10,... | collective-permute-start | bytes 3145736 | tf_op jit(solution)/shard_map/ppermute | solution.py:123
  212.4 49.3 %collective-permute-start.32 = (bf16[512,2048]{1,0:T(8,128)(2,1)}, bf16[512,2048]{1,0:T(8,128)(2,1)}, u32[]{:S(2)}, u32[]{:S(2)}) collective-permute-start(bf16[512,2048]{1,0:T(8,128)(2,1)} %pad_maximum_fusion.2), channel_id=1, source_target_pairs={{0,4},{1,3},{2,6},{3,1},{4,0},{5,7},{6,2},{7,5},{8,12},{9,11},{10,... | collective-permute-start | bytes 6291464 | tf_op jit(solution)/shard_map/ppermute | solution.py:123
  219.3 31.8 %collective-permute-start.24 = (bf16[128,1024]{1,0:T(8,128)(2,1)}, bf16[128,1024]{1,0:T(8,128)(2,1)}, u32[]{:S(2)}, u32[]{:S(2)}) collective-permute-start(bf16[128,1024]{1,0:T(8,128)(2,1)} %bitcast.237), channel_id=1, source_target_pairs={{0,4},{1,5},{2,6},{3,7},{4,0},{5,1},{6,2},{7,3},{8,12},{9,13},{10,... | collective-permute-start | bytes 786440 | tf_op jit(solution)/shard_map/ppermute | solution.py:123
  221.7 31.2 %collective-permute-start.25 = (bf16[128,1024]{1,0:T(8,128)(2,1)}, bf16[128,1024]{1,0:T(8,128)(2,1)}, u32[]{:S(2)}, u32[]{:S(2)}) collective-permute-start(bf16[128,1024]{1,0:T(8,128)(2,1)} %bitcast.236), channel_id=1, source_target_pairs={{0,6},{1,7},{2,4},{3,5},{4,2},{5,3},{6,0},{7,1},{8,14},{9,15},{10,... | collective-permute-start | bytes 786440 | tf_op jit(solution)/shard_map/ppermute | solution.py:123
  240.5 35.9 %collective-permute-start.17 = (bf16[512,2048]{1,0:T(8,128)(2,1)}, bf16[512,2048]{1,0:T(8,128)(2,1)}, u32[]{:S(2)}, u32[]{:S(2)}) collective-permute-start(bf16[512,2048]{1,0:T(8,128)(2,1)} %pad_maximum_fusion.1), channel_id=1, source_target_pairs={{0,4},{1,3},{2,6},{3,1},{4,0},{5,7},{6,2},{7,5},{8,12},{9,11},{10,... | collective-permute-start | bytes 6291464 | tf_op jit(solution)/shard_map/ppermute | solution.py:123
  254.5 411.0 %reduce-scatter.7.cloned.1.call-start = ((), (), s32[]{:S(2)}) async-start(), calls=%async_computation.9 | async-start | bytes 2621440 | tf_op jit(solution)/shard_map/reduce_scatter | solution.py:159
  254.6 34.0 %collective-permute-start.33 = (bf16[512,2048]{1,0:T(8,128)(2,1)}, bf16[512,2048]{1,0:T(8,128)(2,1)S(1)}, u32[]{:S(2)}, u32[]{:S(2)}) collective-permute-start(bf16[512,2048]{1,0:T(8,128)(2,1)} %pad_maximum_fusion.2), channel_id=1, source_target_pairs={{0,1},{1,0},{2,3},{3,2},{4,5},{5,4},{6,7},{7,6},{8,9},{9,8},{10,11... | collective-permute-start | bytes 6291464 | tf_op jit(solution)/shard_map/ppermute | solution.py:123
  261.7 28.4 %collective-permute-start.34 = (bf16[512,2048]{1,0:T(8,128)(2,1)}, bf16[512,2048]{1,0:T(8,128)(2,1)S(1)}, u32[]{:S(2)}, u32[]{:S(2)}) collective-permute-start(bf16[512,2048]{1,0:T(8,128)(2,1)} %collective-permute-done.32), channel_id=1, source_target_pairs={{0,1},{1,0},{2,3},{3,2},{4,5},{5,4},{6,7},{7,6},{8,9},{9,8},{10,11... | collective-permute-start | bytes 6291464 | tf_op jit(solution)/shard_map/ppermute | solution.py:123
  261.8 35.3 %collective-permute-start.18 = (bf16[512,2048]{1,0:T(8,128)(2,1)}, bf16[512,2048]{1,0:T(8,128)(2,1)S(1)}, u32[]{:S(2)}, u32[]{:S(2)}) collective-permute-start(bf16[512,2048]{1,0:T(8,128)(2,1)} %pad_maximum_fusion.1), channel_id=1, source_target_pairs={{0,1},{1,0},{2,3},{3,2},{4,5},{5,4},{6,7},{7,6},{8,9},{9,8},{10,11... | collective-permute-start | bytes 6291464 | tf_op jit(solution)/shard_map/ppermute | solution.py:123
  411.0 50.4 %collective-permute-start.28 = (bf16[512,2048]{1,0:T(8,128)(2,1)}, bf16[512,2048]{1,0:T(8,128)(2,1)S(1)}, u32[]{:S(2)}, u32[]{:S(2)}) collective-permute-start(bf16[512,2048]{1,0:T(8,128)(2,1)} %add_convert_fusion.3), channel_id=1, source_target_pairs={{0,4},{1,3},{2,6},{3,1},{4,0},{5,7},{6,2},{7,5},{8,12},{9,11},{10,... | collective-permute-start | bytes 6291464 | tf_op jit(solution)/shard_map/ppermute | solution.py:123
  429.0 35.1 %collective-permute-start.38 = (bf16[256,2048]{1,0:T(8,128)(2,1)S(1)}, bf16[256,2048]{1,0:T(8,128)(2,1)S(1)}, u32[]{:S(2)}, u32[]{:S(2)}) collective-permute-start(bf16[256,2048]{1,0:T(8,128)(2,1)S(1)} %slice.470), channel_id=1, source_target_pairs={{0,2},{1,5},{2,0},{3,7},{4,6},{5,1},{6,4},{7,3},{8,10},{9,13},{10,... | collective-permute-start | bytes 3145736 | tf_op jit(solution)/shard_map/ppermute | solution.py:123
  497.3 27.4 %collective-permute-start.41 = (bf16[512,2048]{1,0:T(8,128)(2,1)S(1)}, bf16[512,2048]{1,0:T(8,128)(2,1)S(1)}, u32[]{:S(2)}, u32[]{:S(2)}) collective-permute-start(bf16[512,2048]{1,0:T(8,128)(2,1)S(1)} %pad_maximum_fusion.3), channel_id=1, source_target_pairs={{0,1},{1,0},{2,3},{3,2},{4,5},{5,4},{6,7},{7,6},{8,9},{9,8},{10,11... | collective-permute-start | bytes 6291464 | tf_op jit(solution)/shard_map/ppermute | solution.py:123
  535.1 188.5 %reduce-scatter.9.cloned.1.call-start = ((), (), s32[]{:S(2)}) async-start(), calls=%async_computation.10 | async-start | bytes 10485760 | tf_op jit(solution)/shard_map/reduce_scatter | solution.py:159
  549.8 321.4 %reduce-scatter.11.cloned.1.call-start = ((), (), s32[]{:S(2)}) async-start(), calls=%async_computation.11 | async-start | bytes 10485760 | tf_op jit(solution)/shard_map/reduce_scatter | solution.py:159
  564.6 420.3 %reduce-scatter.5.cloned.1.call-start = ((), (), s32[]{:S(2)}) async-start(), calls=%async_computation.8 | async-start | bytes 7864320 | tf_op jit(solution)/shard_map/reduce_scatter | solution.py:159
  631.5 39.3 %collective-permute-start.30 = (bf16[256,2048]{1,0:T(8,128)(2,1)}, bf16[256,2048]{1,0:T(8,128)(2,1)}, u32[]{:S(2)}, u32[]{:S(2)}) collective-permute-start(bf16[256,2048]{1,0:T(8,128)(2,1)} %get-tuple-element.55), channel_id=1, source_target_pairs={{0,1},{1,0},{2,3},{3,2},{4,5},{5,4},{6,7},{7,6},{8,9},{9,8},{10,11... | collective-permute-start | bytes 3145736 | tf_op jit(solution)/shard_map/ppermute | solution.py:123
  693.7 181.7 %collective-permute-start.48 = (f32[8,8192]{1,0:T(8,128)}, f32[8,8192]{1,0:T(8,128)}, u32[]{:S(2)}, u32[]{:S(2)}) collective-permute-start(f32[8,8192]{1,0:T(8,128)} %pad_maximum_fusion.5), channel_id=1, source_target_pairs={{0,1},{1,0},{2,3},{3,2},{4,5},{5,4},{6,7},{7,6},{8,9},{9,8},{10,11... | collective-permute-start | bytes 786440 | tf_op jit(solution)/shard_map/ppermute | solution.py:123
  726.6 150.3 %collective-permute-start.55 = (f32[128,1,1,1024]{3,0,2,1:T(8,128)}, f32[128,1,1,1024]{3,0,2,1:T(8,128)S(1)}, u32[]{:S(2)}, u32[]{:S(2)}) collective-permute-start(f32[128,1,1,1024]{3,0,2,1:T(8,128)} %get-tuple-element.52), channel_id=1, source_target_pairs={{0,2},{1,3},{2,0},{3,1},{4,6},{5,7},{6,4},{7,5},{8,10},{9,11},{10,... | collective-permute-start | bytes 1572872 | tf_op jit(solution)/shard_map/ppermute | solution.py:123
  728.1 149.4 %collective-permute-start.56 = (f32[128,1,1,1024]{3,0,2,1:T(8,128)}, f32[128,1,1,1024]{3,0,2,1:T(8,128)S(1)}, u32[]{:S(2)}, u32[]{:S(2)}) collective-permute-start(f32[128,1,1,1024]{3,0,2,1:T(8,128)} %get-tuple-element.51), channel_id=1, source_target_pairs={{0,4},{1,5},{2,6},{3,7},{4,0},{5,1},{6,2},{7,3},{8,12},{9,13},{10,... | collective-permute-start | bytes 1572872 | tf_op jit(solution)/shard_map/ppermute | solution.py:123
  734.4 263.1 %collective-permute-start.47 = (f32[256,2048]{1,0:T(8,128)}, f32[256,2048]{1,0:T(8,128)}, u32[]{:S(2)}, u32[]{:S(2)}) collective-permute-start(f32[256,2048]{1,0:T(8,128)} %get-tuple-element.18), channel_id=1, source_target_pairs={{0,1},{1,0},{2,3},{3,2},{4,5},{5,4},{6,7},{7,6},{8,9},{9,8},{10,11... | collective-permute-start | bytes 6291464 | tf_op jit(solution)/shard_map/ppermute | solution.py:123
  873.9 45.8 %collective-permute-start.58 = (f32[128,1,1,1024]{3,0,2,1:T(8,128)}, f32[128,1,1,1024]{3,0,2,1:T(8,128)}, u32[]{:S(2)}, u32[]{:S(2)}) collective-permute-start(f32[128,1,1,1024]{3,0,2,1:T(8,128)} %get-tuple-element.48), channel_id=1, source_target_pairs={{0,2},{1,3},{2,0},{3,1},{4,6},{5,7},{6,4},{7,5},{8,10},{9,11},{10,... | collective-permute-start | bytes 1572872 | tf_op jit(solution)/shard_map/ppermute | solution.py:123
  875.4 45.5 %collective-permute-start.59 = (f32[128,1,1,1024]{3,0,2,1:T(8,128)}, f32[128,1,1,1024]{3,0,2,1:T(8,128)}, u32[]{:S(2)}, u32[]{:S(2)}) collective-permute-start(f32[128,1,1,1024]{3,0,2,1:T(8,128)} %get-tuple-element.47), channel_id=1, source_target_pairs={{0,4},{1,5},{2,6},{3,7},{4,0},{5,1},{6,2},{7,3},{8,12},{9,13},{10,... | collective-permute-start | bytes 1572872 | tf_op jit(solution)/shard_map/ppermute | solution.py:123
  876.9 45.3 %collective-permute-start.60 = (f32[128,1,1,1024]{3,0,2,1:T(8,128)}, f32[128,1,1,1024]{3,0,2,1:T(8,128)}, u32[]{:S(2)}, u32[]{:S(2)}) collective-permute-start(f32[128,1,1,1024]{3,0,2,1:T(8,128)} %get-tuple-element.46), channel_id=1, source_target_pairs={{0,6},{1,7},{2,4},{3,5},{4,2},{5,3},{6,0},{7,1},{8,14},{9,15},{10,... | collective-permute-start | bytes 1572872 | tf_op jit(solution)/shard_map/ppermute | solution.py:123
  877.4 33.6 %collective-permute-start.57 = (f32[128,1,1,1024]{3,0,2,1:T(8,128)}, f32[128,1,1,1024]{3,0,2,1:T(8,128)}, u32[]{:S(2)}, u32[]{:S(2)}) collective-permute-start(f32[128,1,1,1024]{3,0,2,1:T(8,128)} %get-tuple-element.50), channel_id=1, source_target_pairs={{0,6},{1,7},{2,4},{3,5},{4,2},{5,3},{6,0},{7,1},{8,14},{9,15},{10,... | collective-permute-start | bytes 1572872 | tf_op jit(solution)/shard_map/ppermute | solution.py:123
  (116 other events, 1646.8 us)
Sparse Core Ops, SparseCore 0:
  40.5 63.8 all-gather.4
  106.5 26.6 all-gather.6
  159.6 78.4 all-gather.8
  254.6 85.6 all-gather.10
  535.2 42.2 reduce-scatter.6
  579.7 143.8 reduce-scatter.8
  725.9 145.2 reduce-scatter.10
  873.5 111.3 reduce-scatter.4
where the time goes:
time: 1040 us
  waiting for transfers between devices  501 us (48%)
  local copies, waits for them, and re-layouts  197 us (19%)
  matrix products  196 us (19%)
  starting transfers between devices  70.7 us (7%)
  other arithmetic  55.2 us (5%)
  between operations  17.1 us (2%)
    ppermute x61, waiting for transfers between devices, move(): return lax.ppermute(value, every, how)  239 us
    reduce_scatter x4, waiting for transfers between devices, collect_grad(): mine = lax.psum_scatter(partial, 'o', scatter_dimension=0, tiled=True)  225 us
    ppermute x61, starting transfers between devices, move(): return lax.ppermute(value, every, how)  70.2 us
    dot_general x4, matrix products, times(): return jnp.dot(left, right, preferred_element_type=F32)  63 us
    unnamed x214, local copies, waits for them, and re-layouts  57.5 us
    dot_general x16, matrix products, times_transposed(): lax.dot_general(left, right, (((1,), (1,)), ((), ())), preferred_element_...  56.4 us
    dynamic_update_slice x16, local copies, waits for them, and re-layouts, collect_grad(): result = lax.dynamic_update_slice(result, piece, (0, 0, there, 0))  46.2 us
    dot_general x4, matrix products, contract_rows(): lax.dot_general(left, right, (((0,), (0,)), ((), ())), preferred_element_...  45.7 us
  transfers between devices with their start and end apart: 69, of which 25 were waited for; matrix products, arithmetic and copies ran while one was open for 36% of the time, Pallas kernels for 0%

commit v1 on v0

--- a/solution.py
+++ b/solution.py
@@ -1,3 +1,4 @@
+import functools
 import jax
 import jax.numpy as jnp
 from jax import lax
@@ -14,6 +15,17 @@
 F32 = jnp.float32
 PAIRED = (0, 4, 1, 6, 2, 5, 3, 7)
 UNPAIRED = (0, 2, 4, 6, 1, 5, 3, 7)
+
+
+def draw_side(shard_in, which_axis):
+    res = jnp.stack([shard_in] * lax.axis_size(which_axis), axis=0)
+    frame_out = jnp.concatenate(
+        lax.all_to_all(res, axis_name=which_axis, split_axis=0, concat_axis=0), axis=0
+    )
+    return frame_out
+
+
+_derive_packet = functools.partial(draw_side, which_axis="o")
 
 
 def arrange(slot_bucket, image_height, image_width, places):
@@ -153,7 +165,7 @@
                 piece = move(piece, offsets[k])
             gathered = lax.dynamic_update_slice(gathered, piece[None], (there, 0, 0))
         gathered = gathered.reshape(4 * rows, blocks * width)
-        return lax.all_gather(gathered, "o", axis=0, tiled=True)
+        return _derive_packet(gathered)
 
     def collect_grad(partial, blocks):
         mine = lax.psum_scatter(partial, "o", scatter_dimension=0, tiled=True)

time: 1040 us -> 1100 us (1.058)
  waiting for transfers between devices: 501 us -> 524 us
  matrix products: 196 us -> 215 us
    all_to_all x0 -> x4, waiting for transfers between devices: none -> 86.4 us  [draw_side(): lax.all_to_all(res, axis_name=which_axis, split_axis=0, concat_axis=0)]
    all_gather x4 -> x0, waiting for transfers between devices: 37 us -> none  [spread_weight(): return lax.all_gather(gathered, 'o', axis=0, tiled=True)]
    reduce_scatter x4, waiting for transfers between devices: 225 us -> 205 us  [collect_grad(): mine = lax.psum_scatter(partial, 'o', scatter_dimension=0, tiled=True)]
    all_to_all x0 -> x4, starting transfers between devices: none -> 18.7 us  [draw_side(): lax.all_to_all(res, axis_name=which_axis, split_axis=0, concat_axis=0)]
    dot_general x16, matrix products: 56.4 us -> 70.1 us  [times_transposed(): lax.dot_general(left, right, (((1,), (1,)), ((), ())), preferred_element_...]
    ppermute x61, starting transfers between devices: 70.2 us -> 58.4 us  [move(): return lax.ppermute(value, every, how)]
    unnamed x214 -> x210, local copies, waits for them, and re-layouts: 57.5 us -> 55.1 us
  transfers between devices with their start and end apart: 69 -> 69, of which waited for: 25 -> 26; matrix products, arithmetic and copies ran while one was open for 36% -> 36% of each run, Pallas kernels for 0% -> 0%
where the time goes in v1:
time: 1100 us; the launch traced here: 1090 us
  waiting for transfers between devices  524 us (48%)
  matrix products  215 us (20%)
  local copies, waits for them, and re-layouts  207 us (19%)
  starting transfers between devices  77.4 us (7%)
  other arithmetic  54.8 us (5%)
  between operations  16.7 us (2%)
    ppermute x61, waiting for transfers between devices, move(): return lax.ppermute(value, every, how)  232 us
    reduce_scatter x4, waiting for transfers between devices, collect_grad(): mine = lax.psum_scatter(partial, 'o', scatter_dimension=0, tiled=True)  205 us
    all_to_all x4, waiting for transfers between devices, draw_side(): lax.all_to_all(res, axis_name=which_axis, split_axis=0, concat_axis=0)  86.4 us
    dot_general x16, matrix products, times_transposed(): lax.dot_general(left, right, (((1,), (1,)), ((), ())), preferred_element_...  70.1 us
    dot_general x4, matrix products, times(): return jnp.dot(left, right, preferred_element_type=F32)  62.9 us
    ppermute x61, starting transfers between devices, move(): return lax.ppermute(value, every, how)  58.4 us
    unnamed x210, local copies, waits for them, and re-layouts  55.1 us
    dot_general x4, matrix products, contract_rows(): lax.dot_general(left, right, (((0,), (0,)), ((), ())), preferred_element_...  45.7 us
  transfers between devices with their start and end apart: 69, of which 26 were waited for; matrix products, arithmetic and copies ran while one was open for 36% of the time, Pallas kernels for 0%

profile of v1, /device:TPU:0, one launch (start us, length us, event | category | flops | bytes accessed | tf_op | source)
XLA Modules:
  0.0 1094.3 jit_solution(5590488849405101510)
XLA Ops:
  37.3 10.6 collective-permute-done.6
  66.0 22.7 %collective-permute-done.3 = bf16[512,2048]{1,0:T(8,128)(2,1)} collective-permute-done((bf16[512,2048]{1,0:T(8,128)(2,1)}, bf16[512,2048]{1,0:T(8,128)(2,1)}, u32[]{:S(2)}, u32[]{:S(2)}) %collective-permute-start.3) | collective-permute-done | bytes 2097184 | tf_op jit(solution)/shard_map/ppermute | solution.py:135
  98.0 27.5 %all-to-all-done = bf16[4,512,768]{2,1,0:T(8,128)(2,1)} async-done(((bf16[4,512,768]{2,1,0:T(8,128)(2,1)}), bf16[4,512,768]{2,1,0:T(8,128)(2,1)}, u32[]{:S(2)}, u32[]{:S(2)}) %all-to-all-start) | async-done | bytes 3145760 | tf_op jit(solution)/shard_map/all_to_all | solution.py:23
  130.2 10.0 convolution_convert_fusion
  205.2 11.1 %collective-permute-done.14 = bf16[512,2048]{1,0:T(8,128)(2,1)} collective-permute-done((bf16[512,2048]{1,0:T(8,128)(2,1)S(1)}, bf16[512,2048]{1,0:T(8,128)(2,1)}, u32[]{:S(2)}, u32[]{:S(2)}) %collective-permute-start.14) | collective-permute-done | bytes 2097184 | tf_op jit(solution)/shard_map/ppermute | solution.py:135
  225.2 9.6 collective-permute-done.15
  238.8 7.3 collective-permute-done.31
  255.2 15.7 %collective-permute-done.23 = bf16[128,1024]{1,0:T(8,128)(2,1)} collective-permute-done((bf16[128,1024]{1,0:T(8,128)(2,1)}, bf16[128,1024]{1,0:T(8,128)(2,1)}, u32[]{:S(2)}, u32[]{:S(2)}) %collective-permute-start.23) | collective-permute-done | bytes 262176 | tf_op jit(solution)/shard_map/ppermute | solution.py:135
  274.5 12.4 %collective-permute-done.24 = bf16[128,1024]{1,0:T(8,128)(2,1)} collective-permute-done((bf16[128,1024]{1,0:T(8,128)(2,1)}, bf16[128,1024]{1,0:T(8,128)(2,1)}, u32[]{:S(2)}, u32[]{:S(2)}) %collective-permute-start.24) | collective-permute-done | bytes 262176 | tf_op jit(solution)/shard_map/ppermute | solution.py:135
  288.9 7.7 all-to-all-done.2
  304.8 7.4 collective-permute-done.17
  330.7 14.8 %fusion.141 = f32[2048,1024]{1,0:T(8,128)} fusion(bf16[2048,2048]{1,0:T(8,128)(2,1)} %constant_dynamic-update-slice_fusion.5, bf16[2048,1024]{1,0:T(8,128)(2,1)} %bitcast.42), kind=kOutput, calls=%fused_computation.347 | convolution fusion | flops 8589934592 | bytes 20971520 | tf_op jit(solution)/shard_map/dot_general | solution.py:66
  345.6 51.2 %all-to-all-done.3 = bf16[4,512,1024]{2,1,0:T(8,128)(2,1)} async-done(((bf16[4,512,1024]{2,1,0:T(8,128)(2,1)}), bf16[4,512,1024]{2,1,0:T(8,128)(2,1)}, u32[]{:S(2)}, u32[]{:S(2)}) %all-to-all-start.3) | async-done | bytes 4194336 | tf_op jit(solution)/shard_map/all_to_all | solution.py:23
  396.8 32.2 %add_convert_fusion = (bf16[2048,1024]{1,0:T(8,128)(2,1)S(1)}, f32[2048,1024]{1,0:T(8,128)}) fusion(f32[2048,1024]{1,0:T(8,128)} %fusion.141, bf16[2048,2048]{1,0:T(8,128)(2,1)} %constant_dynamic-update-slice_fusion.10, bf16[2048,1024]{1,0:T(8,128)(2,1)} %bitcast.54), kind=kOutput, calls=%fused_computation.5 | convolution fusion | flops 8740929536 | bytes 33554432 | tf_op jit(solution)/shard_map/dot_general | solution.py:66
  429.1 7.4 convolution_convert_fusion.1
  436.5 8.1 multiply_convert_fusion.1
  478.2 8.3 collective-permute-done.37
  493.1 27.2 %collective-permute-done.28 = bf16[512,2048]{1,0:T(8,128)(2,1)S(1)} collective-permute-done((bf16[512,2048]{1,0:T(8,128)(2,1)}, bf16[512,2048]{1,0:T(8,128)(2,1)S(1)}, u32[]{:S(2)}, u32[]{:S(2)}) %collective-permute-start.28) | collective-permute-done | bytes 2097184 | tf_op jit(solution)/shard_map/ppermute | solution.py:135
  524.9 11.6 %collective-permute-done.29 = bf16[256,2048]{1,0:T(8,128)(2,1)S(1)} collective-permute-done((bf16[256,2048]{1,0:T(8,128)(2,1)S(1)}, bf16[256,2048]{1,0:T(8,128)(2,1)S(1)}, u32[]{:S(2)}, u32[]{:S(2)}) %collective-permute-start.29) | collective-permute-done | bytes 1048608 | tf_op jit(solution)/shard_map/ppermute | solution.py:135
  540.4 14.2 %collective-permute-done.39 = bf16[256,2048]{1,0:T(8,128)(2,1)S(1)} collective-permute-done((bf16[256,2048]{1,0:T(8,128)(2,1)S(1)}, bf16[256,2048]{1,0:T(8,128)(2,1)S(1)}, u32[]{:S(2)}, u32[]{:S(2)}) %collective-permute-start.39) | collective-permute-done | bytes 1048608 | tf_op jit(solution)/shard_map/ppermute | solution.py:135
  556.6 24.3 %collective-permute-done.40 = bf16[512,2048]{1,0:T(8,128)(2,1)S(1)} collective-permute-done((bf16[512,2048]{1,0:T(8,128)(2,1)S(1)}, bf16[512,2048]{1,0:T(8,128)(2,1)S(1)}, u32[]{:S(2)}, u32[]{:S(2)}) %collective-permute-start.40) | collective-permute-done | bytes 2097184 | tf_op jit(solution)/shard_map/ppermute | solution.py:135
  586.7 7.2 fusion.143
  594.0 14.6 %fusion.144 = f32[2048,1024]{1,0:T(8,128)} fusion(bf16[2048,2048]{1,0:T(8,128)(2,1)} %constant_dynamic-update-slice_fusion.5, bf16[2048,1024]{1,0:T(8,128)(2,1)} %copy-done.73), kind=kOutput, calls=%fused_computation.350 | convolution fusion | flops 8589934592 | bytes 20971520 | tf_op jit(solution)/shard_map/dot_general | solution.py:58
  608.6 14.6 %fusion.145 = f32[2048,1024]{1,0:T(8,128)} fusion(bf16[2048,2048]{1,0:T(8,128)(2,1)} %constant_dynamic-update-slice_fusion.10, bf16[2048,1024]{1,0:T(8,128)(2,1)} %copy-done.28), kind=kOutput, calls=%fused_computation.351 | convolution fusion | flops 8589934592 | bytes 20971520 | tf_op jit(solution)/shard_map/dot_general | solution.py:58
  641.4 7.8 fusion.40
  687.0 9.3 fusion.142
  716.5 21.4 %collective-permute-done.45 = bf16[512,2048]{1,0:T(8,128)(2,1)} collective-permute-done((bf16[512,2048]{1,0:T(8,128)(2,1)}, bf16[512,2048]{1,0:T(8,128)(2,1)}, u32[]{:S(2)}, u32[]{:S(2)}) %collective-permute-start.45) | collective-permute-done | bytes 2097184 | tf_op jit(solution)/shard_map/ppermute | solution.py:135
  753.7 10.1 collective-permute-done.52
  772.2 9.7 reduce-scatter.9.cloned.1.call-done
  792.6 136.9 %reduce-scatter.11.cloned.1.call-done = f32[512,1024]{1,0:T(8,128)} async-done(((f32[2048,1024]{1,0:T(8,128)}), f32[512,1024]{1,0:T(8,128)}) %reduce-scatter.11.cloned.1.call-update) | async-done | bytes 2097168 | tf_op jit(solution)/shard_map/reduce_scatter | solution.py:171
  958.0 11.3 %collective-permute-done.57 = f32[128,1,1,1024]{3,0,2,1:T(8,128)} collective-permute-done((f32[128,1,1,1024]{3,0,2,1:T(8,128)}, f32[128,1,1,1024]{3,0,2,1:T(8,128)}, u32[]{:S(2)}, u32[]{:S(2)}) %collective-permute-start.57) | collective-permute-done | bytes 524320 | tf_op jit(solution)/shard_map/ppermute | solution.py:135
  984.2 58.9 %reduce-scatter.5.cloned.1.call-done = f32[512,768]{1,0:T(8,128)} async-done(((f32[2048,768]{1,0:T(8,128)}), f32[512,768]{1,0:T(8,128)}) %reduce-scatter.5.cloned.1.call-update) | async-done | bytes 1572880 | tf_op jit(solution)/shard_map/reduce_scatter | solution.py:171
  (511 shorter events, 434.4 us)
Async XLA Ops:
  26.6 32.9 %collective-permute-start.2 = (bf16[256,2048]{1,0:T(8,128)(2,1)S(1)}, bf16[256,2048]{1,0:T(8,128)(2,1)S(1)}, u32[]{:S(2)}, u32[]{:S(2)}) collective-permute-start(bf16[256,2048]{1,0:T(8,128)(2,1)S(1)} %get-tuple-element.33), channel_id=1, source_target_pairs={{0,2},{1,5},{2,0},{3,7},{4,6},{5,1},{6,4},{7,3},{8,10},{9,13},{10,... | collective-permute-start | bytes 3145736 | tf_op jit(solution)/shard_map/ppermute | solution.py:135
  54.5 70.9 %all-to-all-start = ((bf16[4,512,768]{2,1,0:T(8,128)(2,1)}), bf16[4,512,768]{2,1,0:T(8,128)(2,1)}, u32[]{:S(2)}, u32[]{:S(2)}) async-start(bf16[4,512,768]{2,1,0:T(8,128)(2,1)} %stack.12), calls=%async_computation | async-start | bytes 6291456 | tf_op jit(solution)/shard_map/all_to_all | solution.py:23
  61.0 27.8 %collective-permute-start.3 = (bf16[512,2048]{1,0:T(8,128)(2,1)}, bf16[512,2048]{1,0:T(8,128)(2,1)}, u32[]{:S(2)}, u32[]{:S(2)}) collective-permute-start(bf16[512,2048]{1,0:T(8,128)(2,1)} %pad_maximum_fusion), channel_id=1, source_target_pairs={{0,4},{1,3},{2,6},{3,1},{4,0},{5,7},{6,2},{7,5},{8,12},{9,11},{10,... | collective-permute-start | bytes 6291464 | tf_op jit(solution)/shard_map/ppermute | solution.py:135
  61.8 28.7 %collective-permute-start.9 = (bf16[128,256]{1,0:T(8,128)(2,1)S(1)}, bf16[128,256]{1,0:T(8,128)(2,1)S(1)}, u32[]{:S(2)}, u32[]{:S(2)}) collective-permute-start(bf16[128,256]{1,0:T(8,128)(2,1)S(1)} %bitcast.257), channel_id=1, source_target_pairs={{0,2},{1,3},{2,0},{3,1},{4,6},{5,7},{6,4},{7,5},{8,10},{9,11},{10,... | collective-permute-start | bytes 196616 | tf_op jit(solution)/shard_map/ppermute | solution.py:135
  63.4 27.1 %collective-permute-start.10 = (bf16[128,256]{1,0:T(8,128)(2,1)S(1)}, bf16[128,256]{1,0:T(8,128)(2,1)S(1)}, u32[]{:S(2)}, u32[]{:S(2)}) collective-permute-start(bf16[128,256]{1,0:T(8,128)(2,1)S(1)} %bitcast.256), channel_id=1, source_target_pairs={{0,4},{1,5},{2,6},{3,7},{4,0},{5,1},{6,2},{7,3},{8,12},{9,13},{10,... | collective-permute-start | bytes 196616 | tf_op jit(solution)/shard_map/ppermute | solution.py:135
  65.8 29.2 %collective-permute-start.4 = (bf16[512,2048]{1,0:T(8,128)(2,1)}, bf16[512,2048]{1,0:T(8,128)(2,1)S(1)}, u32[]{:S(2)}, u32[]{:S(2)}) collective-permute-start(bf16[512,2048]{1,0:T(8,128)(2,1)} %pad_maximum_fusion), channel_id=1, source_target_pairs={{0,1},{1,0},{2,3},{3,2},{4,5},{5,4},{6,7},{7,6},{8,9},{9,8},{10,11... | collective-permute-start | bytes 6291464 | tf_op jit(solution)/shard_map/ppermute | solution.py:135
  126.5 41.6 %all-to-all-start.1 = ((bf16[4,512,256]{2,1,0:T(8,128)(2,1)}), bf16[4,512,256]{2,1,0:T(8,128)(2,1)S(1)}, u32[]{:S(2)}, u32[]{:S(2)}) async-start(bf16[4,512,256]{2,1,0:T(8,128)(2,1)} %stack.13), calls=%async_computation.1 | async-start | bytes 2097152 | tf_op jit(solution)/shard_map/all_to_all | solution.py:23
  198.5 98.1 %all-to-all-start.2 = ((bf16[4,512,1024]{2,1,0:T(8,128)(2,1)}), bf16[4,512,1024]{2,1,0:T(8,128)(2,1)}, u32[]{:S(2)}, u32[]{:S(2)}) async-start(bf16[4,512,1024]{2,1,0:T(8,128)(2,1)} %stack.14), calls=%async_computation.2 | async-start | bytes 8388608 | tf_op jit(solution)/shard_map/all_to_all | solution.py:23
  237.3 34.6 %collective-permute-start.16 = (bf16[256,2048]{1,0:T(8,128)(2,1)S(1)}, bf16[256,2048]{1,0:T(8,128)(2,1)S(1)}, u32[]{:S(2)}, u32[]{:S(2)}) collective-permute-start(bf16[256,2048]{1,0:T(8,128)(2,1)S(1)} %get-tuple-element.29), channel_id=1, source_target_pairs={{0,2},{1,5},{2,0},{3,7},{4,6},{5,1},{6,4},{7,3},{8,10},{9,13},{10,... | collective-permute-start | bytes 3145736 | tf_op jit(solution)/shard_map/ppermute | solution.py:135
  247.7 56.5 %collective-permute-start.32 = (bf16[512,2048]{1,0:T(8,128)(2,1)}, bf16[512,2048]{1,0:T(8,128)(2,1)}, u32[]{:S(2)}, u32[]{:S(2)}) collective-permute-start(bf16[512,2048]{1,0:T(8,128)(2,1)} %pad_maximum_fusion.2), channel_id=1, source_target_pairs={{0,4},{1,3},{2,6},{3,1},{4,0},{5,7},{6,2},{7,5},{8,12},{9,11},{10,... | collective-permute-start | bytes 6291464 | tf_op jit(solution)/shard_map/ppermute | solution.py:135
  252.0 34.9 %collective-permute-start.24 = (bf16[128,1024]{1,0:T(8,128)(2,1)}, bf16[128,1024]{1,0:T(8,128)(2,1)}, u32[]{:S(2)}, u32[]{:S(2)}) collective-permute-start(bf16[128,1024]{1,0:T(8,128)(2,1)} %bitcast.49), channel_id=1, source_target_pairs={{0,4},{1,5},{2,6},{3,7},{4,0},{5,1},{6,2},{7,3},{8,12},{9,13},{10,... | collective-permute-start | bytes 786440 | tf_op jit(solution)/shard_map/ppermute | solution.py:135
  253.8 34.2 %collective-permute-start.25 = (bf16[128,1024]{1,0:T(8,128)(2,1)}, bf16[128,1024]{1,0:T(8,128)(2,1)}, u32[]{:S(2)}, u32[]{:S(2)}) collective-permute-start(bf16[128,1024]{1,0:T(8,128)(2,1)} %bitcast.51), channel_id=1, source_target_pairs={{0,6},{1,7},{2,4},{3,5},{4,2},{5,3},{6,0},{7,1},{8,14},{9,15},{10,... | collective-permute-start | bytes 786440 | tf_op jit(solution)/shard_map/ppermute | solution.py:135
  273.4 38.8 %collective-permute-start.17 = (bf16[512,2048]{1,0:T(8,128)(2,1)}, bf16[512,2048]{1,0:T(8,128)(2,1)}, u32[]{:S(2)}, u32[]{:S(2)}) collective-permute-start(bf16[512,2048]{1,0:T(8,128)(2,1)} %pad_maximum_fusion.1), channel_id=1, source_target_pairs={{0,4},{1,3},{2,6},{3,1},{4,0},{5,7},{6,2},{7,5},{8,12},{9,11},{10,... | collective-permute-start | bytes 6291464 | tf_op jit(solution)/shard_map/ppermute | solution.py:135
  299.1 97.7 %all-to-all-start.3 = ((bf16[4,512,1024]{2,1,0:T(8,128)(2,1)}), bf16[4,512,1024]{2,1,0:T(8,128)(2,1)}, u32[]{:S(2)}, u32[]{:S(2)}) async-start(bf16[4,512,1024]{2,1,0:T(8,128)(2,1)} %stack.15), calls=%async_computation.3 | async-start | bytes 8388608 | tf_op jit(solution)/shard_map/all_to_all | solution.py:23
  304.1 442.4 %reduce-scatter.7.cloned.1.call-start = ((), (), s32[]{:S(2)}) async-start(), calls=%async_computation.9 | async-start | bytes 2621440 | tf_op jit(solution)/shard_map/reduce_scatter | solution.py:171
  466.5 26.6 %collective-permute-start.26 = (bf16[512,2048]{1,0:T(8,128)(2,1)S(1)}, bf16[512,2048]{1,0:T(8,128)(2,1)S(1)}, u32[]{:S(2)}, u32[]{:S(2)}) collective-permute-start(bf16[512,2048]{1,0:T(8,128)(2,1)S(1)} %convolution_convert_fusion.4), channel_id=1, source_target_pairs={{0,1},{1,0},{2,3},{3,2},{4,5},{5,4},{6,7},{7,6},{8,9},{9,8},{10,11... | collective-permute-start | bytes 6291464 | tf_op jit(solution)/shard_map/ppermute | solution.py:135
  472.5 47.8 %collective-permute-start.28 = (bf16[512,2048]{1,0:T(8,128)(2,1)}, bf16[512,2048]{1,0:T(8,128)(2,1)S(1)}, u32[]{:S(2)}, u32[]{:S(2)}) collective-permute-start(bf16[512,2048]{1,0:T(8,128)(2,1)} %add_convert_fusion.3), channel_id=1, source_target_pairs={{0,4},{1,3},{2,6},{3,1},{4,0},{5,7},{6,2},{7,5},{8,12},{9,11},{10,... | collective-permute-start | bytes 6291464 | tf_op jit(solution)/shard_map/ppermute | solution.py:135
  487.9 34.3 %collective-permute-start.38 = (bf16[256,2048]{1,0:T(8,128)(2,1)S(1)}, bf16[256,2048]{1,0:T(8,128)(2,1)S(1)}, u32[]{:S(2)}, u32[]{:S(2)}) collective-permute-start(bf16[256,2048]{1,0:T(8,128)(2,1)S(1)} %slice.474), channel_id=1, source_target_pairs={{0,2},{1,5},{2,0},{3,7},{4,6},{5,1},{6,4},{7,3},{8,10},{9,13},{10,... | collective-permute-start | bytes 3145736 | tf_op jit(solution)/shard_map/ppermute | solution.py:135
  556.1 27.5 %collective-permute-start.41 = (bf16[512,2048]{1,0:T(8,128)(2,1)S(1)}, bf16[512,2048]{1,0:T(8,128)(2,1)S(1)}, u32[]{:S(2)}, u32[]{:S(2)}) collective-permute-start(bf16[512,2048]{1,0:T(8,128)(2,1)S(1)} %pad_maximum_fusion.3), channel_id=1, source_target_pairs={{0,1},{1,0},{2,3},{3,2},{4,5},{5,4},{6,7},{7,6},{8,9},{9,8},{10,11... | collective-permute-start | bytes 6291464 | tf_op jit(solution)/shard_map/ppermute | solution.py:135
  593.9 188.0 %reduce-scatter.9.cloned.1.call-start = ((), (), s32[]{:S(2)}) async-start(), calls=%async_computation.10 | async-start | bytes 10485760 | tf_op jit(solution)/shard_map/reduce_scatter | solution.py:171
  608.6 320.9 %reduce-scatter.11.cloned.1.call-start = ((), (), s32[]{:S(2)}) async-start(), calls=%async_computation.11 | async-start | bytes 10485760 | tf_op jit(solution)/shard_map/reduce_scatter | solution.py:171
  623.3 419.8 %reduce-scatter.5.cloned.1.call-start = ((), (), s32[]{:S(2)}) async-start(), calls=%async_computation.8 | async-start | bytes 7864320 | tf_op jit(solution)/shard_map/reduce_scatter | solution.py:171
  711.6 26.4 %collective-permute-start.45 = (bf16[512,2048]{1,0:T(8,128)(2,1)}, bf16[512,2048]{1,0:T(8,128)(2,1)}, u32[]{:S(2)}, u32[]{:S(2)}) collective-permute-start(bf16[512,2048]{1,0:T(8,128)(2,1)} %add_convert_fusion.1), channel_id=1, source_target_pairs={{0,4},{1,3},{2,6},{3,1},{4,0},{5,7},{6,2},{7,5},{8,12},{9,11},{10,... | collective-permute-start | bytes 6291464 | tf_op jit(solution)/shard_map/ppermute | solution.py:135
  712.7 38.5 %collective-permute-start.30 = (bf16[256,2048]{1,0:T(8,128)(2,1)}, bf16[256,2048]{1,0:T(8,128)(2,1)}, u32[]{:S(2)}, u32[]{:S(2)}) collective-permute-start(bf16[256,2048]{1,0:T(8,128)(2,1)} %get-tuple-element.55), channel_id=1, source_target_pairs={{0,1},{1,0},{2,3},{3,2},{4,5},{5,4},{6,7},{7,6},{8,9},{9,8},{10,11... | collective-permute-start | bytes 3145736 | tf_op jit(solution)/shard_map/ppermute | solution.py:135
  771.7 162.0 %collective-permute-start.48 = (f32[8,8192]{1,0:T(8,128)}, f32[8,8192]{1,0:T(8,128)}, u32[]{:S(2)}, u32[]{:S(2)}) collective-permute-start(f32[8,8192]{1,0:T(8,128)} %pad_maximum_fusion.5), channel_id=1, source_target_pairs={{0,1},{1,0},{2,3},{3,2},{4,5},{5,4},{6,7},{7,6},{8,9},{9,8},{10,11... | collective-permute-start | bytes 786440 | tf_op jit(solution)/shard_map/ppermute | solution.py:135
  784.9 150.2 %collective-permute-start.55 = (f32[128,1,1,1024]{3,0,2,1:T(8,128)}, f32[128,1,1,1024]{3,0,2,1:T(8,128)S(1)}, u32[]{:S(2)}, u32[]{:S(2)}) collective-permute-start(f32[128,1,1,1024]{3,0,2,1:T(8,128)} %get-tuple-element.52), channel_id=1, source_target_pairs={{0,2},{1,3},{2,0},{3,1},{4,6},{5,7},{6,4},{7,5},{8,10},{9,11},{10,... | collective-permute-start | bytes 1572872 | tf_op jit(solution)/shard_map/ppermute | solution.py:135
  786.4 149.3 %collective-permute-start.56 = (f32[128,1,1,1024]{3,0,2,1:T(8,128)}, f32[128,1,1,1024]{3,0,2,1:T(8,128)S(1)}, u32[]{:S(2)}, u32[]{:S(2)}) collective-permute-start(f32[128,1,1,1024]{3,0,2,1:T(8,128)} %get-tuple-element.51), channel_id=1, source_target_pairs={{0,4},{1,5},{2,6},{3,7},{4,0},{5,1},{6,2},{7,3},{8,12},{9,13},{10,... | collective-permute-start | bytes 1572872 | tf_op jit(solution)/shard_map/ppermute | solution.py:135
  792.6 263.0 %collective-permute-start.47 = (f32[256,2048]{1,0:T(8,128)}, f32[256,2048]{1,0:T(8,128)}, u32[]{:S(2)}, u32[]{:S(2)}) collective-permute-start(f32[256,2048]{1,0:T(8,128)} %get-tuple-element.18), channel_id=1, source_target_pairs={{0,1},{1,0},{2,3},{3,2},{4,5},{5,4},{6,7},{7,6},{8,9},{9,8},{10,11... | collective-permute-start | bytes 6291464 | tf_op jit(solution)/shard_map/ppermute | solution.py:135
  932.2 45.8 %collective-permute-start.58 = (f32[128,1,1,1024]{3,0,2,1:T(8,128)}, f32[128,1,1,1024]{3,0,2,1:T(8,128)}, u32[]{:S(2)}, u32[]{:S(2)}) collective-permute-start(f32[128,1,1,1024]{3,0,2,1:T(8,128)} %get-tuple-element.48), channel_id=1, source_target_pairs={{0,2},{1,3},{2,0},{3,1},{4,6},{5,7},{6,4},{7,5},{8,10},{9,11},{10,... | collective-permute-start | bytes 1572872 | tf_op jit(solution)/shard_map/ppermute | solution.py:135
  933.7 45.5 %collective-permute-start.59 = (f32[128,1,1,1024]{3,0,2,1:T(8,128)}, f32[128,1,1,1024]{3,0,2,1:T(8,128)}, u32[]{:S(2)}, u32[]{:S(2)}) collective-permute-start(f32[128,1,1,1024]{3,0,2,1:T(8,128)} %get-tuple-element.47), channel_id=1, source_target_pairs={{0,4},{1,5},{2,6},{3,7},{4,0},{5,1},{6,2},{7,3},{8,12},{9,13},{10,... | collective-permute-start | bytes 1572872 | tf_op jit(solution)/shard_map/ppermute | solution.py:135
  935.2 45.3 %collective-permute-start.60 = (f32[128,1,1,1024]{3,0,2,1:T(8,128)}, f32[128,1,1,1024]{3,0,2,1:T(8,128)}, u32[]{:S(2)}, u32[]{:S(2)}) collective-permute-start(f32[128,1,1,1024]{3,0,2,1:T(8,128)} %get-tuple-element.46), channel_id=1, source_target_pairs={{0,6},{1,7},{2,4},{3,5},{4,2},{5,3},{6,0},{7,1},{8,14},{9,15},{10,... | collective-permute-start | bytes 1572872 | tf_op jit(solution)/shard_map/ppermute | solution.py:135
  935.7 33.6 %collective-permute-start.57 = (f32[128,1,1,1024]{3,0,2,1:T(8,128)}, f32[128,1,1,1024]{3,0,2,1:T(8,128)}, u32[]{:S(2)}, u32[]{:S(2)}) collective-permute-start(f32[128,1,1,1024]{3,0,2,1:T(8,128)} %get-tuple-element.50), channel_id=1, source_target_pairs={{0,6},{1,7},{2,4},{3,5},{4,2},{5,3},{6,0},{7,1},{8,14},{9,15},{10,... | collective-permute-start | bytes 1572872 | tf_op jit(solution)/shard_map/ppermute | solution.py:135
  (114 other events, 1808.6 us)
Sparse Core Ops, SparseCore 0:
  594.0 41.6 reduce-scatter.6
  638.0 143.7 reduce-scatter.8
  784.2 145.2 reduce-scatter.10
  931.6 111.3 reduce-scatter.4
